TPU v7x, 32 devices: a whole 2x2x4 slice. The times are simulated.
32 devices in a mesh: blk: 4 (over y, x), grp: 8 (over z, core).
Axes of the slice: x: 2, y: 2, z: 4, core: 2. Of those that a mesh axis runs over, the one named last changes fastest.
Arguments:
- h_blocks: bfloat16 [1536, 16, 128, 128], P(('blk', 'grp')), may hold values from -0.0625 to 0.0625
- h_cols: int32 [1536, 16], P(('blk', 'grp')), may hold values from 0 to 1535, as said below
- t_prev: bfloat16 [196608, 128], P(('blk', 'grp')), may hold values from -6 to 6
- t_cur: bfloat16 [196608, 128], P(('blk', 'grp')), may hold values from -6 to 6
- cheb_coeffs: float32 [3], replicated, may hold values from 0.4 to 1
- owner_slot: int32 [128], replicated, may hold values from 0 to 127, each once
Outputs:
- t_next: bfloat16 [196608, 128], P(('blk', 'grp'))
- t_last: bfloat16 [196608, 128], P(('blk', 'grp'))
- owner_density: float32 [128, 196608], P(('blk', 'grp'))
Inputs may be any that keep to these rules, and one draw needn't show every extreme that they name: Block column h_cols[i, k] lies within 24 block rows of i, counted around the ends (periodically); distances of exactly 24 occur both ways; a name may repeat within a row. `owner_slot`: each row of the owner layout receives exactly one window column.
All inputs are finite; a program needn't handle non-finite values.
Results may differ from a plain program's by a relative error of at most 0.009.
Values may be sent and summed in bfloat16 or wider, within the bound.
A program may use at most 192 MiB of HBM per device.

v0:
```python
import jax
import jax.numpy as jnp
from jax import lax
from jax.sharding import PartitionSpec as P

NBLK = 1536


def extended_2(array, sides, width):
    for axis, dim in sides:
        size, length = (lax.axis_size(axis), array.shape[dim])
        up = [(i, (i + 1) % size) for i in range(size)]
        down = [(j, i) for i, j in up]
        last = lax.slice_in_dim(array, length - width, length, axis=dim)
        first = lax.slice_in_dim(array, 0, width, axis=dim)
        before = lax.ppermute(last, axis, up)
        after = lax.ppermute(first, axis, down)
        array = jnp.concatenate([before, array, after], axis=dim)
    return array


def apply_band(h_blocks, local_cols, extended, block_order, width):
    blocks = extended.reshape(-1, block_order, width)
    picked = jnp.take(blocks, local_cols, axis=0)
    total = jnp.einsum("rkab,rkbm->ram", h_blocks, picked, preferred_element_type=jnp.float32)
    return total.reshape(-1, width)


def to_owner_rows(columns_major, owner_slot):
    return jnp.zeros_like(columns_major).at[owner_slot].set(columns_major)


def on_device(h_blocks, h_cols, t_prev, t_cur, cheb_coeffs, owner_slot):
    rows_dev = h_blocks.shape[0]
    block_order = h_blocks.shape[2]
    width = t_cur.shape[1]
    reach = rows_dev // 2
    first_row = lax.axis_index(("blk", "grp")) * rows_dev
    local_cols = (h_cols - first_row + reach) % NBLK
    before, current = (t_prev, t_cur)
    made = []
    relayed = None
    for term in range(3):
        extended = extended_2(current, ((("blk", "grp"), 0),), reach * block_order)
        product = apply_band(h_blocks, local_cols, extended, block_order, width)
        fresh = (2.0 * product - before.astype(jnp.float32)).astype(jnp.bfloat16)
        made.append(fresh)
        weighted = to_owner_rows((cheb_coeffs[term] * fresh.astype(jnp.float32)).T, owner_slot)
        arrived = lax.all_to_all(weighted, ("blk", "grp"), split_axis=0, concat_axis=1, tiled=True)
        relayed = arrived if relayed is None else relayed + arrived
        before, current = (current, fresh)
    return (made[1], made[2], relayed)


def solution(mesh):
    return jax.shard_map(
        on_device,
        mesh=mesh,
        in_specs=(
            P(("blk", "grp"), None, None, None),
            P(("blk", "grp"), None),
            P(("blk", "grp"), None),
            P(("blk", "grp"), None),
            P(),
            P(),
        ),
        out_specs=(P(("blk", "grp"), None), P(("blk", "grp"), None), P(("blk", "grp"), None)),
        check_vma=False,
    )
```

profile of v0, /device:TPU:16, one launch (start us, length us, event | category | flops | bytes accessed | tf_op | source)
XLA Modules:
  0.0 320.0 jit_solution(7295205855601659484)
XLA Ops:
  3.6 11.8 %collective-permute-done.1 = bf16[3072,128]{1,0:T(8,128)(2,1)S(1)} collective-permute-done((bf16[3072,128]{1,0:T(8,128)(2,1)S(1)}, bf16[3072,128]{1,0:T(8,128)(2,1)S(1)}, u32[]{:S(2)}, u32[]{:S(2)}) %collective-permute-start.1) | collective-permute-done | bytes 786464 | tf_op jit(solution)/shard_map/ppermute | solution.py:17
  16.3 5.9 %collective-permute-done = bf16[3072,128]{1,0:T(8,128)(2,1)} collective-permute-done((bf16[3072,128]{1,0:T(8,128)(2,1)S(1)}, bf16[3072,128]{1,0:T(8,128)(2,1)}, u32[]{:S(2)}, u32[]{:S(2)}) %collective-permute-start) | collective-permute-done | bytes 786464 | tf_op jit(solution)/shard_map/ppermute | solution.py:16
  22.2 3.9 %pad_maximum_fusion = bf16[12288,128]{1,0:T(8,128)(2,1)S(1)} fusion(bf16[3072,128]{1,0:T(8,128)(2,1)} %copy-done.5, bf16[6144,128]{1,0:T(8,128)(2,1)} %param.11, bf16[3072,128]{1,0:T(8,128)(2,1)} %collective-permute-done), kind=kLoop, calls=%fused_computation.22 | loop fusion | flops 9437184 | bytes 6291456 | tf_op jit(solution)/shard_map/concatenate | solution.py:18
  26.2 19.2 %gather_fusion = bf16[768,128,128]{2,1,0:T(8,128)(2,1)} fusion(bf16[96,128,128]{2,1,0:T(8,128)(2,1)S(1)} %bitcast.54, s32[1024]{0:T(1024)S(1)} %pad_clamp_fusion), kind=kCustom, calls=%fused_computation.clone | custom fusion | bytes 50334720 | tf_op jit(solution)/shard_map/jit(_take)/gather | solution.py:24
  45.4 18.2 %bitcast_multiply_fusion.2 = f32[48,128,128]{1,2,0:T(8,128)S(1)} fusion(bf16[48,16,128,128]{3,2,1,0:T(8,128)(2,1)} %param.8, bf16[48,16,128,128]{3,2,1,0:T(8,128)(2,1)} %bitcast.57, pred[48,16]{1,0:T(8,128)(4,1)S(1)} %copy.16), kind=kOutput, calls=%fused_computation.31 | convolution fusion | flops 3234594816 | bytes 53478144 | tf_op jit(solution)/shard_map/rkab,rkbm->ram/dot_general | solution.py:25
  67.5 2.4 copy.22
  69.8 4.4 %scatter_custom_fusion = f32[128,6144]{1,0:T(8,128)S(1)} fusion(s32[128]{0:T(128)S(1)} %compare_select_fusion.1, f32[128,6144]{1,0:T(8,128)} %copy.22, f32[]{:T(128)} %constant.41.clone.1), kind=kCustom, calls=%fused_computation.39 | custom fusion | bytes 3146240 | tf_op jit(solution)/shard_map/scatter | solution.py:30
  76.4 10.9 %all-to-all-start = ((f32[32,4,6144]{2,1,0:T(4,128)}), f32[32,4,6144]{2,1,0:T(4,128)}, u32[]{:S(2)}, u32[]{:S(2)}) async-start(f32[32,4,6144]{2,1,0:T(4,128)} %all_to_all.30), calls=%async_computation | async-start | bytes 6291456 | tf_op jit(solution)/shard_map/all_to_all | solution.py:49
  87.3 4.0 %pad_maximum_fusion.1 = bf16[12288,128]{1,0:T(8,128)(2,1)S(1)} fusion(bf16[3072,128]{1,0:T(8,128)(2,1)} %collective-permute-done.3, bf16[6144,128]{1,0:T(8,128)(2,1)} %copy-done, bf16[3072,128]{1,0:T(8,128)(2,1)} %collective-permute-done.2), kind=kLoop, calls=%fused_computation.23 | loop fusion | flops 9437184 | bytes 6291456 | tf_op jit(solution)/shard_map/concatenate | solution.py:18
  91.3 19.2 %gather_fusion.1 = bf16[768,128,128]{2,1,0:T(8,128)(2,1)} fusion(bf16[96,128,128]{2,1,0:T(8,128)(2,1)S(1)} %bitcast.55, s32[1024]{0:T(1024)S(1)} %pad_clamp_fusion), kind=kCustom, calls=%fused_computation.1.clone | custom fusion | bytes 50334720 | tf_op jit(solution)/shard_map/jit(_take)/gather | solution.py:24
  110.5 18.2 %bitcast_multiply_fusion.1 = f32[48,128,128]{1,2,0:T(8,128)S(1)} fusion(bf16[48,16,128,128]{3,2,1,0:T(8,128)(2,1)} %param.8, bf16[48,16,128,128]{3,2,1,0:T(8,128)(2,1)} %bitcast.58, pred[48,16]{1,0:T(8,128)(4,1)S(1)} %copy.16), kind=kOutput, calls=%fused_computation.30 | convolution fusion | flops 3234594816 | bytes 53478144 | tf_op jit(solution)/shard_map/rkab,rkbm->ram/dot_general | solution.py:25
  134.9 4.4 %scatter_custom_fusion.1 = f32[128,6144]{1,0:T(8,128)S(1)} fusion(s32[128]{0:T(128)S(1)} %compare_select_fusion.1, f32[128,6144]{1,0:T(8,128)} %copy.23, f32[]{:T(128)} %constant.41.clone.1), kind=kCustom, calls=%fused_computation.37 | custom fusion | bytes 3146240 | tf_op jit(solution)/shard_map/scatter | solution.py:30
  141.4 22.9 %all-to-all-done = f32[32,4,6144]{2,1,0:T(4,128)} async-done(((f32[32,4,6144]{2,1,0:T(4,128)}), f32[32,4,6144]{2,1,0:T(4,128)}, u32[]{:S(2)}, u32[]{:S(2)}) %all-to-all-start) | async-done | bytes 3145760 | tf_op jit(solution)/shard_map/all_to_all | solution.py:49
  164.3 7.4 %all-to-all-start.1 = ((f32[32,4,6144]{2,1,0:T(4,128)}), f32[32,4,6144]{2,1,0:T(4,128)}, u32[]{:S(2)}, u32[]{:S(2)}) async-start(f32[32,4,6144]{2,1,0:T(4,128)} %all_to_all.32), calls=%async_computation.1 | async-start | bytes 6291456 | tf_op jit(solution)/shard_map/all_to_all | solution.py:49
  173.1 8.3 %collective-permute-done.4 = bf16[3072,128]{1,0:T(8,128)(2,1)} collective-permute-done((bf16[3072,128]{1,0:T(8,128)(2,1)}, bf16[3072,128]{1,0:T(8,128)(2,1)}, u32[]{:S(2)}, u32[]{:S(2)}) %collective-permute-start.4) | collective-permute-done | bytes 786464 | tf_op jit(solution)/shard_map/ppermute | solution.py:16
  181.4 3.9 %pad_maximum_fusion.2 = bf16[12288,128]{1,0:T(8,128)(2,1)S(1)} fusion(bf16[3072,128]{1,0:T(8,128)(2,1)} %collective-permute-done.5, bf16[6144,128]{1,0:T(8,128)(2,1)} %copy-done.3, bf16[3072,128]{1,0:T(8,128)(2,1)} %collective-permute-done.4), kind=kLoop, calls=%fused_computation.24 | loop fusion | flops 9437184 | bytes 6291456 | tf_op jit(solution)/shard_map/concatenate | solution.py:18
  185.4 19.2 %gather_fusion.2 = bf16[768,128,128]{2,1,0:T(8,128)(2,1)} fusion(bf16[96,128,128]{2,1,0:T(8,128)(2,1)S(1)} %bitcast.53, s32[1024]{0:T(1024)S(1)} %pad_clamp_fusion), kind=kCustom, calls=%fused_computation.2.clone | custom fusion | bytes 50334720 | tf_op jit(solution)/shard_map/jit(_take)/gather | solution.py:24
  204.6 18.2 %bitcast_multiply_fusion = f32[48,128,128]{1,2,0:T(8,128)S(1)} fusion(bf16[48,16,128,128]{3,2,1,0:T(8,128)(2,1)} %param.8, bf16[48,16,128,128]{3,2,1,0:T(8,128)(2,1)} %bitcast.56, pred[48,16]{1,0:T(8,128)(4,1)S(1)} %copy.16), kind=kOutput, calls=%fused_computation.29 | convolution fusion | flops 3234594816 | bytes 53478144 | tf_op jit(solution)/shard_map/rkab,rkbm->ram/dot_general | solution.py:25
  224.9 2.4 copy.24
  227.2 5.4 %scatter_custom_fusion.2 = f32[128,6144]{1,0:T(8,128)} fusion(s32[128]{0:T(128)S(1)} %compare_select_fusion.1, f32[128,6144]{1,0:T(8,128)} %copy.24, f32[]{:T(128)} %constant.41.clone.1), kind=kCustom, calls=%fused_computation.35 | custom fusion | bytes 3146240 | tf_op jit(solution)/shard_map/scatter | solution.py:30
  232.7 3.0 all_to_all.34
  235.7 4.9 %all-to-all-done.1 = f32[32,4,6144]{2,1,0:T(4,128)} async-done(((f32[32,4,6144]{2,1,0:T(4,128)}), f32[32,4,6144]{2,1,0:T(4,128)}, u32[]{:S(2)}, u32[]{:S(2)}) %all-to-all-start.1) | async-done | bytes 3145760 | tf_op jit(solution)/shard_map/all_to_all | solution.py:49
  240.7 74.2 %all_to_all.39 = f32[32,4,6144]{2,1,0:T(4,128)S(1)} all-to-all(f32[32,4,6144]{2,1,0:T(4,128)S(1)} %all_to_all.34), channel_id=1, replica_groups=mesh['blk'=4,'grp'=8] {'blk','grp'}, dimensions={0} | all-to-all | bytes 6291456 | tf_op jit(solution)/shard_map/all_to_all | solution.py:49
  314.9 5.1 %add_add_fusion = f32[16,8,6144]{2,1,0:T(8,128)} fusion(f32[16,8,6144]{2,1,0:T(8,128)S(1)} %bitcast.59, f32[16,8,6144]{2,1,0:T(8,128)} %bitcast.50, f32[16,8,6144]{2,1,0:T(8,128)} %bitcast.51), kind=kLoop, calls=%fused_computation.33 | loop fusion | flops 1572864 | bytes 12582912 | tf_op jit(solution)/shard_map/add | solution.py:50
  (43 shorter events, 21.7 us)
Async XLA Ops:
  0.6 2.1 copy-start.6
  0.6 2.4 copy-start.7
  2.1 13.3 %collective-permute-start.1 = (bf16[3072,128]{1,0:T(8,128)(2,1)S(1)}, bf16[3072,128]{1,0:T(8,128)(2,1)S(1)}, u32[]{:S(2)}, u32[]{:S(2)}) collective-permute-start(bf16[3072,128]{1,0:T(8,128)(2,1)S(1)} %get-tuple-element.17), channel_id=1, source_target_pairs={{1,0},{2,1},{3,2},{4,3},{5,4},{6,5},{7,6},{8,7},{9,8},{10,9},{11,1... | collective-permute-start | bytes 2359304 | tf_op jit(solution)/shard_map/ppermute | solution.py:17
  2.2 20.0 %collective-permute-start = (bf16[3072,128]{1,0:T(8,128)(2,1)S(1)}, bf16[3072,128]{1,0:T(8,128)(2,1)}, u32[]{:S(2)}, u32[]{:S(2)}) collective-permute-start(bf16[3072,128]{1,0:T(8,128)(2,1)S(1)} %get-tuple-element.16), channel_id=1, source_target_pairs={{0,1},{1,2},{2,3},{3,4},{4,5},{5,6},{6,7},{7,8},{8,9},{9,10},{10,1... | collective-permute-start | bytes 2359304 | tf_op jit(solution)/shard_map/ppermute | solution.py:16
  15.4 0.9 copy-start.5
  45.4 18.2 %copy-start.4 = (bf16[6144,128]{1,0:T(8,128)(2,1)S(1)}, bf16[6144,128]{1,0:T(8,128)(2,1)}, u32[]{:S(2)}) copy-start(bf16[6144,128]{1,0:T(8,128)(2,1)} %param.10) | copy-start | bytes 4718596
  64.6 1.1 copy-start
  64.6 2.9 copy-start.8
  67.0 20.3 %collective-permute-start.3 = (bf16[3072,128]{1,0:T(8,128)(2,1)}, bf16[3072,128]{1,0:T(8,128)(2,1)}, u32[]{:S(2)}, u32[]{:S(2)}) collective-permute-start(bf16[3072,128]{1,0:T(8,128)(2,1)} %get-tuple-element.15), channel_id=1, source_target_pairs={{1,0},{2,1},{3,2},{4,3},{5,4},{6,5},{7,6},{8,7},{9,8},{10,9},{11,1... | collective-permute-start | bytes 2359304 | tf_op jit(solution)/shard_map/ppermute | solution.py:17
  67.0 20.3 %collective-permute-start.2 = (bf16[3072,128]{1,0:T(8,128)(2,1)}, bf16[3072,128]{1,0:T(8,128)(2,1)}, u32[]{:S(2)}, u32[]{:S(2)}) collective-permute-start(bf16[3072,128]{1,0:T(8,128)(2,1)} %get-tuple-element.14), channel_id=1, source_target_pairs={{0,1},{1,2},{2,3},{3,4},{4,5},{5,6},{6,7},{7,8},{8,9},{9,10},{10,1... | collective-permute-start | bytes 2359304 | tf_op jit(solution)/shard_map/ppermute | solution.py:16
  76.4 87.9 %all-to-all-start = ((f32[32,4,6144]{2,1,0:T(4,128)}), f32[32,4,6144]{2,1,0:T(4,128)}, u32[]{:S(2)}, u32[]{:S(2)}) async-start(f32[32,4,6144]{2,1,0:T(4,128)} %all_to_all.30), calls=%async_computation | async-start | bytes 6291456 | tf_op jit(solution)/shard_map/all_to_all | solution.py:49
  110.5 18.2 %copy-start.2 = (bf16[6144,128]{1,0:T(8,128)(2,1)S(1)}, bf16[6144,128]{1,0:T(8,128)(2,1)}, u32[]{:S(2)}) copy-start(bf16[6144,128]{1,0:T(8,128)(2,1)} %param.11) | copy-start | bytes 4718596
  129.6 1.1 copy-start.3
  132.0 41.1 %collective-permute-start.5 = (bf16[3072,128]{1,0:T(8,128)(2,1)}, bf16[3072,128]{1,0:T(8,128)(2,1)}, u32[]{:S(2)}, u32[]{:S(2)}) collective-permute-start(bf16[3072,128]{1,0:T(8,128)(2,1)} %get-tuple-element.13), channel_id=1, source_target_pairs={{1,0},{2,1},{3,2},{4,3},{5,4},{6,5},{7,6},{8,7},{9,8},{10,9},{11,1... | collective-permute-start | bytes 2359304 | tf_op jit(solution)/shard_map/ppermute | solution.py:17
  132.3 49.1 %collective-permute-start.4 = (bf16[3072,128]{1,0:T(8,128)(2,1)}, bf16[3072,128]{1,0:T(8,128)(2,1)}, u32[]{:S(2)}, u32[]{:S(2)}) collective-permute-start(bf16[3072,128]{1,0:T(8,128)(2,1)} %get-tuple-element.12), channel_id=1, source_target_pairs={{0,1},{1,2},{2,3},{3,4},{4,5},{5,6},{6,7},{7,8},{8,9},{9,10},{10,1... | collective-permute-start | bytes 2359304 | tf_op jit(solution)/shard_map/ppermute | solution.py:16
  164.3 76.3 %all-to-all-start.1 = ((f32[32,4,6144]{2,1,0:T(4,128)}), f32[32,4,6144]{2,1,0:T(4,128)}, u32[]{:S(2)}, u32[]{:S(2)}) async-start(f32[32,4,6144]{2,1,0:T(4,128)} %all_to_all.32), calls=%async_computation.1 | async-start | bytes 6291456 | tf_op jit(solution)/shard_map/all_to_all | solution.py:49
  204.6 18.2 %copy-start.1 = (bf16[6144,128]{1,0:T(8,128)(2,1)S(1)}, bf16[6144,128]{1,0:T(8,128)(2,1)}, u32[]{:S(2)}) copy-start(bf16[6144,128]{1,0:T(8,128)(2,1)} %copy-done) | copy-start | bytes 4718596
where the time goes:
time: 326 us; the launch traced here: 320 us
  local copies, waits for them, and re-layouts  94.2 us (29%)
  blocking collectives  74.2 us (23%)
  waiting for transfers between devices  55.2 us (17%)
  matrix products  54.5 us (17%)
  other arithmetic  21.2 us (7%)
  starting transfers between devices  19.9 us (6%)
    all_to_all x1, blocking collectives, on_device(): lax.all_to_all(weighted, ('blk', 'grp'), split_axis=0, concat_axis=1, til...  74.2 us
    gather x3, local copies, waits for them, and re-layouts, apply_band(): picked = jnp.take(blocks, local_cols, axis=0)  57.6 us
    dot_general x3, matrix products, apply_band(): jnp.einsum('rkab,rkbm->ram', h_blocks, picked, preferred_element_type=jnp...  54.5 us
    all_to_all x2, waiting for transfers between devices, on_device(): lax.all_to_all(weighted, ('blk', 'grp'), split_axis=0, concat_axis=1, til...  27.8 us
    all_to_all x2, starting transfers between devices, on_device(): lax.all_to_all(weighted, ('blk', 'grp'), split_axis=0, concat_axis=1, til...  18.3 us
    scatter x3, local copies, waits for them, and re-layouts, to_owner_rows(): return jnp.zeros_like(columns_major).at[owner_slot].set(columns_major)  14.3 us
    ppermute x3, waiting for transfers between devices, extended_2(): before = lax.ppermute(last, axis, up)  14.3 us
    ppermute x3, waiting for transfers between devices, extended_2(): after = lax.ppermute(first, axis, down)  13.1 us
  transfers between devices with their start and end apart: 8, of which 6 were waited for; matrix products, arithmetic and copies ran while one was open for 34% of the time, Pallas kernels for 0%

commit v1 on v0

v1 whole, which is shorter than its diff:
```python
import functools

import jax
import jax.numpy as jnp
from jax import lax
from jax.experimental import pallas as pl
from jax.experimental.pallas import tpu as pltpu
from jax.sharding import PartitionSpec as P

AXES = ("blk", "grp")


def row_product(cols, row, slots, h_row, ext):
    rhs = jnp.concatenate([ext[cols[row * slots + k]] for k in range(slots)], axis=0)
    lhs = jnp.concatenate([h_row(k) for k in range(slots)], axis=1)
    return jnp.dot(lhs, rhs, preferred_element_type=jnp.float32)


def term_kernel(group, slots, cols, h_ref, prev_ref, before, cur, after, out_ref, ext, sems):
    step = pl.program_id(0)
    reach, rows = before.shape[0], cur.shape[0]

    @pl.when(step == 0)
    def _():
        copies = [
            pltpu.make_async_copy(before, ext.at[pl.ds(0, reach)], sems.at[0]),
            pltpu.make_async_copy(cur, ext.at[pl.ds(reach, rows)], sems.at[1]),
            pltpu.make_async_copy(after, ext.at[pl.ds(reach + rows, reach)], sems.at[2]),
        ]
        for c in copies:
            c.start()
        for c in copies:
            c.wait()

    for r in range(group):
        total = row_product(cols, step * group + r, slots, lambda k: h_ref[r, k], ext)
        out_ref[r] = (2.0 * total - prev_ref[r].astype(jnp.float32)).astype(out_ref.dtype)


def apply_term(cols, h_blocks, prev, before, cur, after):
    rows, slots, bs, _ = h_blocks.shape
    width = cur.shape[2]
    reach = before.shape[0]
    group = 4 if rows % 4 == 0 else 1
    anyspec = pl.BlockSpec(memory_space=pl.ANY)
    return pl.pallas_call(
        functools.partial(term_kernel, group, slots),
        out_shape=jax.ShapeDtypeStruct(cur.shape, cur.dtype),
        grid_spec=pltpu.PrefetchScalarGridSpec(
            num_scalar_prefetch=1,
            grid=(rows // group,),
            in_specs=[
                pl.BlockSpec((group, slots, bs, bs), lambda i, c: (i, 0, 0, 0)),
                pl.BlockSpec((group, bs, width), lambda i, c: (i, 0, 0)),
                anyspec,
                anyspec,
                anyspec,
            ],
            out_specs=pl.BlockSpec((group, bs, width), lambda i, c: (i, 0, 0)),
            scratch_shapes=[
                pltpu.VMEM((rows + 2 * reach, bs, width), cur.dtype),
                pltpu.SemaphoreType.DMA((3,)),
            ],
        ),
        name="term",
    )(cols, h_blocks, prev, before, cur, after)


def fill_chooser(chooser, owner, per_dev, group):
    shape = chooser.shape
    width = shape[1] // group
    q = lax.broadcasted_iota(jnp.int32, shape, 0)
    j = lax.broadcasted_iota(jnp.int32, shape, 1)
    span = group * per_dev
    slot = (q // span) * per_dev + q % per_dev
    hit = ((q % span) // per_dev == j // width) & (slot == owner)
    chooser[...] = jnp.where(hit, 1.0, 0.0).astype(chooser.dtype)


def pack_kernel(group, per_dev, coeffs, owner, a_ref, b_ref, c_ref, out_ref, chooser):
    @pl.when(pl.program_id(0) == 0)
    def _():
        fill_chooser(chooser, owner[...], per_dev, group)

    parts = []
    for b in range(group):
        dens = coeffs[0] * a_ref[b].astype(jnp.float32)
        dens = dens + coeffs[1] * b_ref[b].astype(jnp.float32)
        dens = dens + coeffs[2] * c_ref[b].astype(jnp.float32)
        parts.append(dens.astype(jnp.bfloat16))
    dens = jnp.concatenate(parts, axis=1)
    packed = lax.dot_general(chooser[...], dens, (((1,), (1,)), ((), ())), preferred_element_type=jnp.float32)
    out_ref[...] = packed.reshape(out_ref.shape).astype(out_ref.dtype)


def pack_group(rows, per_dev):
    group = max(1, 16 // per_dev)
    return group if rows % group == 0 else rows


def pack_density(coeffs, owner_slot, made, devices):
    rows, bs, width = made[0].shape
    per_dev = width // devices
    group = pack_group(rows, per_dev)
    tspec = pl.BlockSpec((group, bs, width), lambda i, c: (i, 0, 0))
    return pl.pallas_call(
        functools.partial(pack_kernel, group, per_dev),
        out_shape=jax.ShapeDtypeStruct((devices, rows * per_dev, bs), jnp.bfloat16),
        grid_spec=pltpu.PrefetchScalarGridSpec(
            num_scalar_prefetch=1,
            grid=(rows // group,),
            in_specs=[pl.BlockSpec((1, group * width), lambda i, c: (0, 0)), tspec, tspec, tspec],
            out_specs=pl.BlockSpec((devices, group * per_dev, bs), lambda i, c: (0, i, 0)),
            scratch_shapes=[pltpu.VMEM((devices * group * per_dev, group * width), jnp.bfloat16)],
        ),
        name="pack",
    )(coeffs, jnp.tile(owner_slot, group)[None, :], *made)


def on_device(h_blocks, h_cols, t_prev, t_cur, cheb_coeffs, owner_slot):
    rows, slots, bs, _ = h_blocks.shape
    width = t_cur.shape[1]
    devices = lax.axis_size(AXES)
    reach = rows // 2
    first_row = lax.axis_index(AXES) * rows
    local_cols = ((h_cols - first_row + reach) % (rows * devices)).reshape(-1)
    up = [(i, (i + 1) % devices) for i in range(devices)]
    down = [(j, i) for i, j in up]
    before, current = (t_prev.reshape(rows, bs, width), t_cur.reshape(rows, bs, width))
    made = []
    for _ in range(3):
        left = lax.ppermute(current[rows - reach :], AXES, up)
        right = lax.ppermute(current[:reach], AXES, down)
        fresh = apply_term(local_cols, h_blocks, before, left, current, right)
        made.append(fresh)
        before, current = (current, fresh)
    packed = pack_density(cheb_coeffs, owner_slot, made, devices)
    arrived = lax.all_to_all(packed, AXES, split_axis=0, concat_axis=0, tiled=True)
    per_dev = width // devices
    owned = arrived.astype(jnp.float32).reshape(devices * rows, per_dev, bs)
    owned = owned.transpose(1, 0, 2).reshape(per_dev, devices * rows * bs)
    return (made[1].reshape(-1, width), made[2].reshape(-1, width), owned)


def solution(mesh):
    return jax.shard_map(
        on_device,
        mesh=mesh,
        in_specs=(
            P(("blk", "grp"), None, None, None),
            P(("blk", "grp"), None),
            P(("blk", "grp"), None),
            P(("blk", "grp"), None),
            P(),
            P(),
        ),
        out_specs=(P(("blk", "grp"), None), P(("blk", "grp"), None), P(("blk", "grp"), None)),
        check_vma=False,
    )
```

time: 326 us -> 189 us (0.58)
  the two profiles are of different devices: /device:TPU:16 before, /device:TPU:0 now
where the time goes in v1:
time: 189 us; the launch traced here: 187 us
  Pallas kernels  67.9 us (36%)
  waiting for transfers between devices  49.1 us (26%)
  blocking collectives  44.6 us (24%)
  starting transfers between devices  13.4 us (7%)
  local copies, waits for them, and re-layouts  9.54 us (5%)
  other arithmetic  2.04 us (1%)
    pallas_call x3, Pallas kernels, apply_term(): pl.pallas_call(functools.partial(term_kernel, group, slots), out_shape=ja...  57.1 us
    all_to_all x1, blocking collectives, on_device(): lax.all_to_all(packed, AXES, split_axis=0, concat_axis=0, tiled=True)  44.6 us
    ppermute x3, waiting for transfers between devices, on_device(): right = lax.ppermute(current[:reach], AXES, down)  30.8 us
    ppermute x3, waiting for transfers between devices, on_device(): left = lax.ppermute(current[rows - reach:], AXES, up)  18.3 us
    ppermute x3, starting transfers between devices, on_device(): right = lax.ppermute(current[:reach], AXES, down)  12.9 us
    pallas_call x1, Pallas kernels, pack_density(): pl.pallas_call(functools.partial(pack_kernel, group, per_dev), out_shape=...  10.8 us
    slice x3, local copies, waits for them, and re-layouts, on_device(): right = lax.ppermute(current[:reach], AXES, down)  4.56 us
  transfers between devices with their start and end apart: 6, of which 5 were waited for; matrix products, arithmetic and copies ran while one was open for 0% of the time, Pallas kernels for 0%

profile of v1, /device:TPU:0, one launch (start us, length us, event | category | flops | bytes accessed | tf_op | source)
XLA Modules:
  0.0 187.3 jit_solution(7644162232840719846)
XLA Ops:
  0.6 1.5 fusion.2
  2.1 0.5 collective-permute-start
  2.7 6.0 %collective-permute-start.1 = (bf16[24,128,128]{2,1,0:T(8,128)(2,1)S(1)}, bf16[24,128,128]{2,1,0:T(8,128)(2,1)S(1)}, u32[]{:S(2)}, u32[]{:S(2)}) collective-permute-start(bf16[24,128,128]{2,1,0:T(8,128)(2,1)S(1)} %bitcast.21), channel_id=1, source_target_pairs={{1,0},{2,1},{3,2},{4,3},{5,4},{6,5},{7,6},{8,7},{9,8},{10,9},{11,1... | collective-permute-start | bytes 2359304 | tf_op jit(solution)/shard_map/ppermute | solution.py:133
  8.7 0.7 reshape.34.cols
  9.4 14.7 %collective-permute-done.before = bf16[24,128,128]{2,1,0:T(8,128)(2,1)S(1)} collective-permute-done((bf16[24,128,128]{2,1,0:T(8,128)(2,1)S(1)}, bf16[24,128,128]{2,1,0:T(8,128)(2,1)S(1)}, u32[]{:S(2)}, u32[]{:S(2)}) %collective-permute-start) | collective-permute-done | bytes 786464 | tf_op jit(solution)/shard_map/ppermute | solution.py:132
  24.1 0.9 copy-done
  25.0 0.3 copy-done.1
  25.2 19.0 %term.3.cur.prev_ref.a_ref = bf16[48,128,128]{2,1,0:T(8,128)(2,1)} custom-call(s32[768]{0:T(1024)} %reshape.34.cols, bf16[48,16,128,128]{3,2,1,0:T(8,128)(2,1)} %h_ref.5, bf16[48,128,128]{2,1,0:T(8,128)(2,1)} %bitcast.20, bf16[24,128,128]{2,1,0:T(8,128)(2,1)} %copy-done, bf16[48,128,128]{2,1,0:T(8,128)(2,1)} %bitcast.16, bf16[24,128,128]{2,1,0:T(8,128)(2,1)} %copy-done.1), custom_call_target="tpu_custom_call" | custom-call | tf_op jit(solution)/shard_map/term/pallas_call | solution.py:46
  44.2 1.5 fusion.1
  45.8 3.9 %collective-permute-start.3 = (bf16[24,128,128]{2,1,0:T(8,128)(2,1)S(1)}, bf16[24,128,128]{2,1,0:T(8,128)(2,1)S(1)}, u32[]{:S(2)}, u32[]{:S(2)}) collective-permute-start(bf16[24,128,128]{2,1,0:T(8,128)(2,1)S(1)} %get-tuple-element.5), channel_id=1, source_target_pairs={{1,0},{2,1},{3,2},{4,3},{5,4},{6,5},{7,6},{8,7},{9,8},{10,9},{11,1... | collective-permute-start | bytes 2359304 | tf_op jit(solution)/shard_map/ppermute | solution.py:133
  49.7 16.0 %collective-permute-done.3.after = bf16[24,128,128]{2,1,0:T(8,128)(2,1)S(1)} collective-permute-done((bf16[24,128,128]{2,1,0:T(8,128)(2,1)S(1)}, bf16[24,128,128]{2,1,0:T(8,128)(2,1)S(1)}, u32[]{:S(2)}, u32[]{:S(2)}) %collective-permute-start.3) | collective-permute-done | bytes 786464 | tf_op jit(solution)/shard_map/ppermute | solution.py:133
  65.7 3.5 %collective-permute-done.2.before = bf16[24,128,128]{2,1,0:T(8,128)(2,1)S(1)} collective-permute-done((bf16[24,128,128]{2,1,0:T(8,128)(2,1)S(1)}, bf16[24,128,128]{2,1,0:T(8,128)(2,1)S(1)}, u32[]{:S(2)}, u32[]{:S(2)}) %collective-permute-start.2) | collective-permute-done | bytes 786464 | tf_op jit(solution)/shard_map/ppermute | solution.py:132
  69.1 0.9 copy-done.5
  70.0 19.0 %term.4.cur.b_ref = bf16[48,128,128]{2,1,0:T(8,128)(2,1)} custom-call(s32[768]{0:T(1024)} %reshape.34.cols, bf16[48,16,128,128]{3,2,1,0:T(8,128)(2,1)} %h_ref.5, bf16[48,128,128]{2,1,0:T(8,128)(2,1)} %bitcast.17, bf16[24,128,128]{2,1,0:T(8,128)(2,1)} %copy-done.5, bf16[48,128,128]{2,1,0:T(8,128)(2,1)} %term.3.cur.prev_ref.a_ref, bf16[24,128,128]{2,1,0:T(8,128)(2,1)} %copy-done.3), custom_call_target="tpu_custom_call" | custom-call | tf_op jit(solution)/shard_map/term/pallas_call | solution.py:46
  89.1 1.5 fusion
  90.6 3.0 %collective-permute-start.5 = (bf16[24,128,128]{2,1,0:T(8,128)(2,1)S(1)}, bf16[24,128,128]{2,1,0:T(8,128)(2,1)S(1)}, u32[]{:S(2)}, u32[]{:S(2)}) collective-permute-start(bf16[24,128,128]{2,1,0:T(8,128)(2,1)S(1)} %get-tuple-element.3), channel_id=1, source_target_pairs={{1,0},{2,1},{3,2},{4,3},{5,4},{6,5},{7,6},{8,7},{9,8},{10,9},{11,1... | collective-permute-start | bytes 2359304 | tf_op jit(solution)/shard_map/ppermute | solution.py:133
  93.6 14.8 %collective-permute-done.5.after = bf16[24,128,128]{2,1,0:T(8,128)(2,1)S(1)} collective-permute-done((bf16[24,128,128]{2,1,0:T(8,128)(2,1)S(1)}, bf16[24,128,128]{2,1,0:T(8,128)(2,1)S(1)}, u32[]{:S(2)}, u32[]{:S(2)}) %collective-permute-start.5) | collective-permute-done | bytes 786464 | tf_op jit(solution)/shard_map/ppermute | solution.py:133
  108.6 0.7 copy-done.2
  109.3 0.9 copy-done.4
  110.2 19.0 %term.5.c_ref = bf16[48,128,128]{2,1,0:T(8,128)(2,1)} custom-call(s32[768]{0:T(1024)} %reshape.34.cols, bf16[48,16,128,128]{3,2,1,0:T(8,128)(2,1)} %h_ref.5, bf16[48,128,128]{2,1,0:T(8,128)(2,1)} %term.3.cur.prev_ref.a_ref, bf16[24,128,128]{2,1,0:T(8,128)(2,1)} %copy-done.4, bf16[48,128,128]{2,1,0:T(8,128)(2,1)} %term.4.cur.b_ref, ...), custom_call_target="tpu_custom_call" | custom-call | tf_op jit(solution)/shard_map/term/pallas_call | solution.py:46
  129.3 0.6 tile.2
  129.9 10.8 %pack.1 = bf16[32,192,128]{2,1,0:T(8,128)(2,1)} custom-call(f32[3]{0:T(128)} %coeffs.1, s32[1,512]{1,0:T(1,128)} %bitcast.23, bf16[48,128,128]{2,1,0:T(8,128)(2,1)} %term.3.cur.prev_ref.a_ref, bf16[48,128,128]{2,1,0:T(8,128)(2,1)} %term.4.cur.b_ref, bf16[48,128,128]{2,1,0:T(8,128)(2,1)} %term.5.c_ref), custom_call_target="tpu_custom_call" | custom-call | tf_op jit(solution)/shard_map/pack/pallas_call | solution.py:106
  140.7 44.6 %all_to_all.5 = bf16[32,192,128]{2,1,0:T(8,128)(2,1)S(1)} all-to-all(bf16[32,192,128]{2,1,0:T(8,128)(2,1)} %pack.1), channel_id=1, replica_groups=mesh['blk'=4,'grp'=8] {'blk','grp'}, dimensions={0} | all-to-all | bytes 3145728 | tf_op jit(solution)/shard_map/all_to_all | solution.py:138
  185.3 2.0 %convert.6 = f32[32,192,128]{2,1,0:T(8,128)} convert(bf16[32,192,128]{2,1,0:T(8,128)(2,1)S(1)} %all_to_all.5) | non-fusion elementwise | flops 786432 | bytes 4718592
  (17 shorter events, 0.3 us)
Async XLA Ops:
  0.6 8.0 %copy-start.6 = (s32[48,16]{0,1:T(8,128)S(1)}, s32[48,16]{0,1:T(8,128)}, u32[]{:S(2)}) copy-start(s32[48,16]{0,1:T(8,128)} %param.7) | copy-start | bytes 9220
  2.1 22.0 %collective-permute-start = (bf16[24,128,128]{2,1,0:T(8,128)(2,1)S(1)}, bf16[24,128,128]{2,1,0:T(8,128)(2,1)S(1)}, u32[]{:S(2)}, u32[]{:S(2)}) collective-permute-start(bf16[24,128,128]{2,1,0:T(8,128)(2,1)S(1)} %bitcast.22), channel_id=1, source_target_pairs={{0,1},{1,2},{2,3},{3,4},{4,5},{5,6},{6,7},{7,8},{8,9},{9,10},{10,1... | collective-permute-start | bytes 2359304 | tf_op jit(solution)/shard_map/ppermute | solution.py:132
  2.7 21.4 %collective-permute-start.1 = (bf16[24,128,128]{2,1,0:T(8,128)(2,1)S(1)}, bf16[24,128,128]{2,1,0:T(8,128)(2,1)S(1)}, u32[]{:S(2)}, u32[]{:S(2)}) collective-permute-start(bf16[24,128,128]{2,1,0:T(8,128)(2,1)S(1)} %bitcast.21), channel_id=1, source_target_pairs={{1,0},{2,1},{3,2},{4,3},{5,4},{6,5},{7,6},{8,7},{9,8},{10,9},{11,1... | collective-permute-start | bytes 2359304 | tf_op jit(solution)/shard_map/ppermute | solution.py:133
  24.1 0.9 copy-start
  24.1 1.1 copy-start.1
  45.8 19.9 %collective-permute-start.3 = (bf16[24,128,128]{2,1,0:T(8,128)(2,1)S(1)}, bf16[24,128,128]{2,1,0:T(8,128)(2,1)S(1)}, u32[]{:S(2)}, u32[]{:S(2)}) collective-permute-start(bf16[24,128,128]{2,1,0:T(8,128)(2,1)S(1)} %get-tuple-element.5), channel_id=1, source_target_pairs={{1,0},{2,1},{3,2},{4,3},{5,4},{6,5},{7,6},{8,7},{9,8},{10,9},{11,1... | collective-permute-start | bytes 2359304 | tf_op jit(solution)/shard_map/ppermute | solution.py:133
  49.7 19.4 %collective-permute-start.2 = (bf16[24,128,128]{2,1,0:T(8,128)(2,1)S(1)}, bf16[24,128,128]{2,1,0:T(8,128)(2,1)S(1)}, u32[]{:S(2)}, u32[]{:S(2)}) collective-permute-start(bf16[24,128,128]{2,1,0:T(8,128)(2,1)S(1)} %get-tuple-element.6), channel_id=1, source_target_pairs={{0,1},{1,2},{2,3},{3,4},{4,5},{5,6},{6,7},{7,8},{8,9},{9,10},{10,1... | collective-permute-start | bytes 2359304 | tf_op jit(solution)/shard_map/ppermute | solution.py:132
  65.7 3.5 %copy-start.3 = (bf16[24,128,128]{2,1,0:T(8,128)(2,1)}, bf16[24,128,128]{2,1,0:T(8,128)(2,1)S(1)}, u32[]{:S(2)}) copy-start(bf16[24,128,128]{2,1,0:T(8,128)(2,1)S(1)} %collective-permute-done.3.after) | copy-start | bytes 2359300
  69.1 0.9 copy-start.5
  90.6 17.8 %collective-permute-start.5 = (bf16[24,128,128]{2,1,0:T(8,128)(2,1)S(1)}, bf16[24,128,128]{2,1,0:T(8,128)(2,1)S(1)}, u32[]{:S(2)}, u32[]{:S(2)}) collective-permute-start(bf16[24,128,128]{2,1,0:T(8,128)(2,1)S(1)} %get-tuple-element.3), channel_id=1, source_target_pairs={{1,0},{2,1},{3,2},{4,3},{5,4},{6,5},{7,6},{8,7},{9,8},{10,9},{11,1... | collective-permute-start | bytes 2359304 | tf_op jit(solution)/shard_map/ppermute | solution.py:133
  93.6 35.7 %copy-start.7 = (s32[128]{0:T(128)S(1)}, s32[128]{0:T(128)}, u32[]{:S(2)}) copy-start(s32[128]{0:T(128)} %param.11) | copy-start | bytes 1540
  93.6 15.0 %collective-permute-start.4 = (bf16[24,128,128]{2,1,0:T(8,128)(2,1)S(1)}, bf16[24,128,128]{2,1,0:T(8,128)(2,1)S(1)}, u32[]{:S(2)}, u32[]{:S(2)}) collective-permute-start(bf16[24,128,128]{2,1,0:T(8,128)(2,1)S(1)} %get-tuple-element.4), channel_id=1, source_target_pairs={{0,1},{1,2},{2,3},{3,4},{4,5},{5,6},{6,7},{7,8},{8,9},{9,10},{10,1... | collective-permute-start | bytes 2359304 | tf_op jit(solution)/shard_map/ppermute | solution.py:132
  108.4 0.9 copy-start.2
  109.3 0.9 copy-start.4

commit v2 on v0

v2 whole, which is shorter than its diff:
```python
import functools

import jax
import jax.numpy as jnp
from jax import lax
from jax.experimental import pallas as pl
from jax.experimental.pallas import tpu as pltpu
from jax.sharding import PartitionSpec as P

AXES = ("blk", "grp")

MESH = pl.DeviceIdType.MESH


def row_product(cols, row, h_ref, ext):
    slots = h_ref.shape[1]
    rhs = jnp.concatenate([ext[cols[row * slots + k]] for k in range(slots)], axis=0)
    lhs = jnp.concatenate([h_ref[row, k] for k in range(slots)], axis=1)
    return jnp.dot(lhs, rhs, preferred_element_type=jnp.float32)


def whole_kernel(
    shape, cols, coeffs, owner, h_hbm, prev_hbm, cur_hbm, next_out, last_out, arrived,
    h_ref, ext_a, ext_b, ext_c, prev_ref, last_ref, packed, stage, chooser,
    load_sem, h_sem, send_sem, recv_sem, spread_sem, gather_sem, out_sem,
):
    reach, pieces, per_dev, group = shape
    rows, _, bs, width = h_ref.shape[0], h_ref.shape[1], h_ref.shape[2], ext_a.shape[2]
    piece = reach // pieces
    blks, grps = lax.axis_size("blk"), lax.axis_size("grp")
    devices = blks * grps
    blk, grp = lax.axis_index("blk"), lax.axis_index("grp")
    me = blk * grps + grp

    def place(linear):
        return (linear // grps, linear % grps)

    def base_of(c):
        return (c % 2) * reach + (c // 2) * piece

    def h_load(c):
        where = pl.ds(base_of(c), piece)
        return pltpu.make_async_copy(h_hbm.at[where], h_ref.at[where], h_sem.at[c])

    def halo(term, source, offset, dest, c):
        side = c % 2
        there = (1 - side) * (reach + rows) + (c // 2) * piece
        return pltpu.make_async_remote_copy(
            src_ref=source.at[pl.ds(offset + base_of(c), piece)],
            dst_ref=dest.at[pl.ds(there, piece)],
            send_sem=send_sem.at[term, c],
            recv_sem=recv_sem.at[term, c],
            device_id=place((me + devices - 1 + 2 * side) % devices),
            device_id_type=MESH,
        )

    prev_load = pltpu.make_async_copy(prev_hbm, prev_ref, load_sem.at[0])
    cur_load = pltpu.make_async_copy(cur_hbm, ext_a.at[pl.ds(reach, rows)], load_sem.at[1])
    cur_load.start()
    prev_load.start()

    barrier = pltpu.get_barrier_semaphore()

    def greet(i, carry):
        pl.semaphore_signal(barrier, inc=1, device_id=place((me + i) % devices), device_id_type=MESH)
        return carry

    lax.fori_loop(1, devices, greet, 0)
    for c in range(2 * pieces):
        h_load(c).start()

    q = lax.broadcasted_iota(jnp.int32, chooser.shape, 0)
    slot = (q % devices) * per_dev + q // devices
    chooser[...] = jnp.where(slot == owner[...], 1.0, 0.0).astype(chooser.dtype)

    pl.semaphore_wait(barrier, devices - 1)
    for c in range(2 * pieces):
        halo(0, cur_hbm, 0, ext_a, c).start()
    prev_load.wait()
    cur_load.wait()

    def run_term(term, ext, old, old_at, new, new_at, ready, done):
        for c in range(2 * pieces):
            if term == 0:
                halo(0, cur_hbm, 0, ext_a, c).wait()
            else:
                halo(term, ext, reach, ext, c).wait()

        def one_piece(c, carry):
            base = base_of(c)
            ready(c)

            def one_row(r, inner):
                row = base + r
                total = row_product(cols, row, h_ref, ext)
                fresh = 2.0 * total - old[old_at + row].astype(jnp.float32)
                new[new_at + row] = fresh.astype(new.dtype)
                return inner

            lax.fori_loop(0, piece, one_row, 0)
            done(c)
            return carry

        lax.fori_loop(0, 2 * pieces, one_piece, 0)

    def nothing(c):
        pass

    run_term(
        0, ext_a, prev_ref, 0, ext_b, reach,
        lambda c: h_load(c).wait(), lambda c: halo(1, ext_b, reach, ext_b, c).start(),
    )
    run_term(
        1, ext_b, ext_a, reach, ext_c, reach,
        nothing, lambda c: halo(2, ext_c, reach, ext_c, c).start(),
    )
    next_store = pltpu.make_async_copy(ext_c.at[pl.ds(reach, rows)], next_out, out_sem.at[0])
    next_store.start()

    def pack(first):
        for b in range(group):
            row = first + b
            dens = coeffs[0] * ext_b[reach + row].astype(jnp.float32)
            dens = dens + coeffs[1] * ext_c[reach + row].astype(jnp.float32)
            dens = dens + coeffs[2] * last_ref[row].astype(jnp.float32)
            turned = lax.dot_general(
                chooser[...], dens.astype(jnp.bfloat16), (((1,), (1,)), ((), ())),
                preferred_element_type=jnp.float32,
            )
            for s in range(per_dev):
                stage[pl.ds(b * per_dev + s, devices, stride=group * per_dev), :] = turned[
                    s * devices : (s + 1) * devices
                ]
        span = group * per_dev
        tiles = stage[...].reshape(devices, span, bs).astype(packed.dtype)
        packed[:, pl.ds(pl.multiple_of(first * per_dev, span), span), :] = tiles

    def spread(base, count):
        where = pl.ds(base * per_dev, count * per_dev)

        def one(i, carry):
            k = i // blks
            turn = (grps // 2 + (1 - 2 * (k % 2)) * ((k + 1) // 2) + grps) % grps
            to_blk = (blk + i + 1) % blks
            to_grp = (grp + turn) % grps
            pltpu.make_async_remote_copy(
                src_ref=packed.at[to_blk * grps + to_grp, where],
                dst_ref=arrived.at[me, where],
                send_sem=spread_sem,
                recv_sem=gather_sem,
                device_id=(to_blk, to_grp),
                device_id_type=MESH,
            ).start()
            return carry

        lax.fori_loop(0, devices - 1, one, 0)

    interleaved = piece % group == 0

    def last_done(c):
        if interleaved:
            base = base_of(c)

            def one_group(g, carry):
                pack(base + g * group)
                return carry

            lax.fori_loop(0, piece // group, one_group, 0)
            spread(base, piece)

    run_term(2, ext_c, ext_b, reach, last_ref, 0, nothing, last_done)
    last_store = pltpu.make_async_copy(last_ref, last_out, out_sem.at[1])
    last_store.start()
    if not interleaved:
        for g in range(rows // group):
            pack(g * group)
        spread(0, rows)
    own = pltpu.make_async_copy(packed.at[me], arrived.at[me], out_sem.at[2])
    own.start()
    everything = pltpu.make_async_remote_copy(
        src_ref=packed.at[pl.ds(0, devices - 1)],
        dst_ref=arrived.at[pl.ds(0, devices - 1)],
        send_sem=spread_sem,
        recv_sem=gather_sem,
        device_id=place((me + 1) % devices),
        device_id_type=MESH,
    )
    everything.wait()
    own.wait()
    next_store.wait()
    last_store.wait()


def on_device(h_blocks, h_cols, t_prev, t_cur, cheb_coeffs, owner_slot):
    rows, slots, bs, _ = h_blocks.shape
    width = t_cur.shape[1]
    devices = lax.axis_size(AXES)
    reach = rows // 2
    per_dev = width // devices
    pieces = 3 if reach % 3 == 0 else 1
    group = max(1, 16 // per_dev)
    group = group if rows % group == 0 else rows
    first_row = lax.axis_index(AXES) * rows
    local_cols = ((h_cols - first_row + reach) % (rows * devices)).reshape(-1)
    anyspec = pl.BlockSpec(memory_space=pl.ANY)
    smem = pl.BlockSpec(memory_space=pltpu.SMEM)
    vmem = pl.BlockSpec(memory_space=pltpu.VMEM)
    dma = pltpu.SemaphoreType.DMA
    term = jax.ShapeDtypeStruct((rows, bs, width), t_cur.dtype)
    ext = pltpu.VMEM((rows + 2 * reach, bs, width), t_cur.dtype)
    own = pltpu.VMEM((rows, bs, width), t_cur.dtype)
    made_next, made_last, arrived = pl.pallas_call(
        functools.partial(whole_kernel, (reach, pieces, per_dev, group)),
        out_shape=(term, term, jax.ShapeDtypeStruct((devices, rows * per_dev, bs), jnp.bfloat16)),
        in_specs=[smem, smem, vmem, anyspec, anyspec, anyspec],
        out_specs=(anyspec, anyspec, anyspec),
        scratch_shapes=[
            pltpu.VMEM(h_blocks.shape, h_blocks.dtype),
            ext,
            ext,
            ext,
            own,
            own,
            pltpu.VMEM((devices, rows * per_dev, bs), jnp.bfloat16),
            pltpu.VMEM((devices * group * per_dev, bs), jnp.float32),
            pltpu.VMEM((width, width), jnp.bfloat16),
            dma((2,)),
            dma((2 * pieces,)),
            dma((3, 2 * pieces)),
            dma((3, 2 * pieces)),
            dma,
            dma,
            dma((3,)),
        ],
        compiler_params=pltpu.CompilerParams(collective_id=0, has_side_effects=True, vmem_limit_bytes=58 * 1024 * 1024),
        name="whole",
    )(
        local_cols,
        cheb_coeffs,
        owner_slot[None, :],
        h_blocks,
        t_prev.reshape(rows, bs, width),
        t_cur.reshape(rows, bs, width),
    )
    owned = arrived.astype(jnp.float32).reshape(devices * rows, per_dev, bs)
    owned = owned.transpose(1, 0, 2).reshape(per_dev, devices * rows * bs)
    return (made_next.reshape(-1, width), made_last.reshape(-1, width), owned)


def solution(mesh):
    return jax.shard_map(
        on_device,
        mesh=mesh,
        in_specs=(
            P(("blk", "grp"), None, None, None),
            P(("blk", "grp"), None),
            P(("blk", "grp"), None),
            P(("blk", "grp"), None),
            P(),
            P(),
        ),
        out_specs=(P(("blk", "grp"), None), P(("blk", "grp"), None), P(("blk", "grp"), None)),
        check_vma=False,
    )
```

time: 326 us -> 118 us (0.36); the launches traced: 320 us -> 116 us
  Pallas kernels: 0 us -> 107 us
  local copies, waits for them, and re-layouts: 94.2 us -> 3.87 us
  blocking collectives: 74.2 us -> 0 us
  waiting for transfers between devices: 55.2 us -> 0 us
  matrix products: 54.5 us -> 0 us
  starting transfers between devices: 19.9 us -> 0 us
  other arithmetic: 21.2 us -> 4.27 us
    pallas_call x0 -> x1, Pallas kernels: none -> 107 us  [on_device(): pl.pallas_call(functools.partial(whole_kernel, (reach, pieces, per_dev, g...]
    all_to_all x1 -> x0, blocking collectives: 74.2 us -> none  [on_device(): lax.all_to_all(weighted, ('blk', 'grp'), split_axis=0, concat_axis=1, til...]
    gather x3 -> x0, local copies, waits for them, and re-layouts: 57.6 us -> none  [apply_band(): picked = jnp.take(blocks, local_cols, axis=0)]
    dot_general x3 -> x0, matrix products: 54.5 us -> none  [apply_band(): jnp.einsum('rkab,rkbm->ram', h_blocks, picked, preferred_element_type=jnp...]
    all_to_all x2 -> x0, waiting for transfers between devices: 27.8 us -> none  [on_device(): lax.all_to_all(weighted, ('blk', 'grp'), split_axis=0, concat_axis=1, til...]
    ppermute x6 -> x0, waiting for transfers between devices: 27.4 us -> none  [the longest x3 14.3 us: extended_2(): before = lax.ppermute(last, axis, up)]
    all_to_all x2 -> x0, starting transfers between devices: 18.3 us -> none  [on_device(): lax.all_to_all(weighted, ('blk', 'grp'), split_axis=0, concat_axis=1, til...]
    scatter x3 -> x0, local copies, waits for them, and re-layouts: 14.3 us -> none  [to_owner_rows(): return jnp.zeros_like(columns_major).at[owner_slot].set(columns_major)]
  transfers between devices with their start and end apart: 8 -> 0, of which waited for: 6 -> 0; matrix products, arithmetic and copies ran while one was open for 34% -> 0% of each run, Pallas kernels for 0% -> 0%
where the time goes in v2:
time: 118 us; the launch traced here: 116 us
  Pallas kernels  107 us (91%)
  other arithmetic  4.27 us (4%)
  local copies, waits for them, and re-layouts  3.87 us (3%)
    pallas_call x1, Pallas kernels, on_device(): pl.pallas_call(functools.partial(whole_kernel, (reach, pieces, per_dev, g...  107 us
    unnamed x1, other arithmetic  3.55 us
    unnamed x6, local copies, waits for them, and re-layouts  3.12 us

profile of v2, /device:TPU:16, one launch (start us, length us, event | category | flops | bytes accessed | tf_op | source)
XLA Modules:
  0.0 116.1 jit_solution(13889577337874848607)
XLA Ops:
  0.6 0.7 add_select_fusion
  1.3 0.1 copy.10
  1.4 0.7 reshape.31.cols
  2.1 107.3 %whole.1 = (bf16[48,128,128]{2,1,0:T(8,128)(2,1)}, bf16[48,128,128]{2,1,0:T(8,128)(2,1)}, bf16[32,192,128]{2,1,0:T(8,128)(2,1)}) custom-call(s32[768]{0:T(1024)} %reshape.31.cols, f32[3]{0:T(128)} %coeffs.1, s32[1,128]{1,0:T(1,128)} %bitcast.18, bf16[48,16,128,128]{3,2,1,0:T(8,128)(2,1)} %h_hbm.1, bf16[48,128,128]{2,1,0:T(8,128)(2,1)} %bitcast.14, ...), custom_call_target="tpu_custom_call" | custom-call | tf_op jit(solution)/shard_map/whole/pallas_call | solution.py:212
  109.5 0.0 copy-start.1
  109.5 3.6 %convert.6 = f32[32,192,128]{2,1,0:T(8,128)} convert(bf16[32,192,128]{2,1,0:T(8,128)(2,1)} %get-tuple-element.8) | non-fusion elementwise | flops 786432 | bytes 4718592
  113.0 0.0 copy-done.1
  113.0 0.0 copy-start
  113.0 1.1 copy.14
  114.2 0.8 copy-done
  115.0 1.1 copy.15
Async XLA Ops:
  109.5 3.6 %copy-start.1 = (bf16[48,128,128]{2,1,0:T(8,128)(2,1)S(1)}, bf16[48,128,128]{2,1,0:T(8,128)(2,1)}, u32[]{:S(2)}) copy-start(bf16[48,128,128]{2,1,0:T(8,128)(2,1)} %get-tuple-element.6) | copy-start | bytes 4718596
  113.0 2.0 %copy-start = (bf16[48,128,128]{2,1,0:T(8,128)(2,1)S(1)}, bf16[48,128,128]{2,1,0:T(8,128)(2,1)}, u32[]{:S(2)}) copy-start(bf16[48,128,128]{2,1,0:T(8,128)(2,1)} %get-tuple-element.7) | copy-start | bytes 4718596

commit v3 on v2

--- a/solution.py
+++ b/solution.py
@@ -14,14 +14,14 @@
 
 def row_product(cols, row, h_ref, ext):
     slots = h_ref.shape[1]
-    rhs = jnp.concatenate([ext[cols[row * slots + k]] for k in range(slots)], axis=0)
+    rhs = jnp.concatenate([ext[cols[row, k]] for k in range(slots)], axis=0)
     lhs = jnp.concatenate([h_ref[row, k] for k in range(slots)], axis=1)
     return jnp.dot(lhs, rhs, preferred_element_type=jnp.float32)
 
 
 def whole_kernel(
-    shape, cols, coeffs, owner, h_hbm, prev_hbm, cur_hbm, next_out, last_out, arrived,
-    h_ref, ext_a, ext_b, ext_c, prev_ref, last_ref, packed, stage, chooser,
+    shape, h_cols, coeffs, owner, h_hbm, prev_hbm, cur_hbm, next_out, last_out, arrived,
+    h_ref, ext_a, ext_b, ext_c, prev_ref, last_ref, packed, stage, chooser, cols,
     load_sem, h_sem, send_sem, recv_sem, spread_sem, gather_sem, out_sem,
 ):
     reach, pieces, per_dev, group = shape
@@ -35,21 +35,26 @@
     def place(linear):
         return (linear // grps, linear % grps)
 
+    first_side = grp % 2
+
+    def side_of(c):
+        return (first_side + c // pieces) % 2
+
     def base_of(c):
-        return (c % 2) * reach + (c // 2) * piece
+        return side_of(c) * reach + (c % pieces) * piece
 
     def h_load(c):
         where = pl.ds(base_of(c), piece)
         return pltpu.make_async_copy(h_hbm.at[where], h_ref.at[where], h_sem.at[c])
 
     def halo(term, source, offset, dest, c):
-        side = c % 2
-        there = (1 - side) * (reach + rows) + (c // 2) * piece
+        side = side_of(c)
+        there = (1 - side) * (reach + rows) + (c % pieces) * piece
         return pltpu.make_async_remote_copy(
             src_ref=source.at[pl.ds(offset + base_of(c), piece)],
             dst_ref=dest.at[pl.ds(there, piece)],
-            send_sem=send_sem.at[term, c],
-            recv_sem=recv_sem.at[term, c],
+            send_sem=send_sem.at[term, side, c % pieces],
+            recv_sem=recv_sem.at[term, side, c % pieces],
             device_id=place((me + devices - 1 + 2 * side) % devices),
             device_id_type=MESH,
         )
@@ -76,6 +81,17 @@
     pl.semaphore_wait(barrier, devices - 1)
     for c in range(2 * pieces):
         halo(0, cur_hbm, 0, ext_a, c).start()
+    total_rows = rows * devices
+
+    def local_row(row, carry):
+        for k in range(h_ref.shape[1]):
+            at = h_cols[row, k] - me * rows + reach
+            at = jnp.where(at < 0, at + total_rows, at)
+            at = jnp.where(at >= total_rows, at - total_rows, at)
+            cols[row, k] = jnp.clip(at, 0, rows + 2 * reach - 1)
+        return carry
+
+    lax.fori_loop(0, rows, local_row, 0)
     prev_load.wait()
     cur_load.wait()
 
@@ -90,14 +106,11 @@
             base = base_of(c)
             ready(c)
 
-            def one_row(r, inner):
+            for r in range(piece):
                 row = base + r
                 total = row_product(cols, row, h_ref, ext)
                 fresh = 2.0 * total - old[old_at + row].astype(jnp.float32)
                 new[new_at + row] = fresh.astype(new.dtype)
-                return inner
-
-            lax.fori_loop(0, piece, one_row, 0)
             done(c)
             return carry
 
@@ -155,7 +168,7 @@
 
         lax.fori_loop(0, devices - 1, one, 0)
 
-    interleaved = piece % group == 0
+    interleaved = piece % group == 0 and pieces % 2 == 0
 
     def last_done(c):
         if interleaved:
@@ -166,7 +179,10 @@
                 return carry
 
             lax.fori_loop(0, piece // group, one_group, 0)
-            spread(base, piece)
+
+            @pl.when(c % 2 == 1)
+            def _():
+                spread(base - piece, 2 * piece)
 
     run_term(2, ext_c, ext_b, reach, last_ref, 0, nothing, last_done)
     last_store = pltpu.make_async_copy(last_ref, last_out, out_sem.at[1])
@@ -197,12 +213,11 @@
     devices = lax.axis_size(AXES)
     reach = rows // 2
     per_dev = width // devices
-    pieces = 3 if reach % 3 == 0 else 1
+    pieces = next(p for p in (6, 3, 2, 1) if reach % p == 0)
     group = max(1, 16 // per_dev)
     group = group if rows % group == 0 else rows
-    first_row = lax.axis_index(AXES) * rows
-    local_cols = ((h_cols - first_row + reach) % (rows * devices)).reshape(-1)
     anyspec = pl.BlockSpec(memory_space=pl.ANY)
+    hbm = pl.BlockSpec(memory_space=pltpu.HBM)
     smem = pl.BlockSpec(memory_space=pltpu.SMEM)
     vmem = pl.BlockSpec(memory_space=pltpu.VMEM)
     dma = pltpu.SemaphoreType.DMA
@@ -212,7 +227,7 @@
     made_next, made_last, arrived = pl.pallas_call(
         functools.partial(whole_kernel, (reach, pieces, per_dev, group)),
         out_shape=(term, term, jax.ShapeDtypeStruct((devices, rows * per_dev, bs), jnp.bfloat16)),
-        in_specs=[smem, smem, vmem, anyspec, anyspec, anyspec],
+        in_specs=[smem, smem, vmem, hbm, hbm, hbm],
         out_specs=(anyspec, anyspec, anyspec),
         scratch_shapes=[
             pltpu.VMEM(h_blocks.shape, h_blocks.dtype),
@@ -224,23 +239,24 @@
             pltpu.VMEM((devices, rows * per_dev, bs), jnp.bfloat16),
             pltpu.VMEM((devices * group * per_dev, bs), jnp.float32),
             pltpu.VMEM((width, width), jnp.bfloat16),
+            pltpu.SMEM((rows, slots), jnp.int32),
             dma((2,)),
             dma((2 * pieces,)),
-            dma((3, 2 * pieces)),
-            dma((3, 2 * pieces)),
+            dma((3, 2, pieces)),
+            dma((3, 2, pieces)),
             dma,
             dma,
             dma((3,)),
         ],
-        compiler_params=pltpu.CompilerParams(collective_id=0, has_side_effects=True, vmem_limit_bytes=58 * 1024 * 1024),
+        compiler_params=pltpu.CompilerParams(collective_id=0, has_side_effects=True, vmem_limit_bytes=42 * 1024 * 1024),
         name="whole",
     )(
-        local_cols,
+        h_cols,
         cheb_coeffs,
         owner_slot[None, :],
         h_blocks,
-        t_prev.reshape(rows, bs, width),
-        t_cur.reshape(rows, bs, width),
+        pltpu.with_memory_space_constraint(t_prev.reshape(rows, bs, width), pltpu.HBM),
+        pltpu.with_memory_space_constraint(t_cur.reshape(rows, bs, width), pltpu.HBM),
     )
     owned = arrived.astype(jnp.float32).reshape(devices * rows, per_dev, bs)
     owned = owned.transpose(1, 0, 2).reshape(per_dev, devices * rows * bs)

time: 118 us -> 109 us (0.924); the launches traced: 116 us -> 109 us
  Pallas kernels: 107 us -> 102 us
  other arithmetic: 4.27 us -> 2.03 us
    pallas_call x1, Pallas kernels: 107 us -> 102 us  [on_device(): pl.pallas_call(functools.partial(whole_kernel, (reach, pieces, per_dev, g...]
    unnamed x1, other arithmetic: 3.55 us -> 2.03 us
    unnamed x6 -> x7, local copies, waits for them, and re-layouts: 3.12 us -> 4.37 us
where the time goes in v3:
time: 109 us
  Pallas kernels  102 us (94%)
  local copies, waits for them, and re-layouts  4.37 us (4%)
  other arithmetic  2.03 us (2%)
    pallas_call x1, Pallas kernels, on_device(): pl.pallas_call(functools.partial(whole_kernel, (reach, pieces, per_dev, g...  102 us
    unnamed x7, local copies, waits for them, and re-layouts  4.37 us

profile of v3, /device:TPU:16, one launch (start us, length us, event | category | flops | bytes accessed | tf_op | source)
XLA Modules:
  0.0 109.1 jit_solution(7769000397893888476)
XLA Ops:
  0.6 0.8 copy.9.h_cols
  1.4 0.0 copy-start
  1.4 0.7 copy-done
  2.1 0.0 copy-start.1
  2.1 0.7 copy-done.1
  2.7 102.1 %whole.1 = (bf16[48,128,128]{2,1,0:T(8,128)(2,1)S(1)}, bf16[48,128,128]{2,1,0:T(8,128)(2,1)S(1)}, bf16[32,192,128]{2,1,0:T(8,128)(2,1)S(1)}) custom-call(s32[48,16]{1,0:T(8,128)S(1)} %copy.9.h_cols, f32[3]{0:T(128)S(1)} %copy-done, s32[1,128]{1,0:T(1,128)S(1)} %bitcast.15, bf16[48,16,128,128]{3,2,1,0:T(8,128)(2,1)} %h_hbm.1, bf16[48,128,128]{2,1,0:T(8,128)(2,1)} %bitcast.17, ...), custom_call_target="tpu_custom_call" | custom-call | tf_op jit(solution)/shard_map/whole/pallas_call | solution.py:227
  104.8 2.0 %convert.6 = f32[32,192,128]{2,1,0:T(8,128)} convert(bf16[32,192,128]{2,1,0:T(8,128)(2,1)S(1)} %get-tuple-element.8) | non-fusion elementwise | flops 786432 | bytes 4718592
  106.8 1.1 %copy.13 = bf16[6144,128]{1,0:T(8,128)(2,1)} copy(bf16[6144,128]{1,0:T(8,128)(2,1)S(1)} %bitcast.14) | data formatting | bytes 3145728
  108.0 1.1 %copy.14 = bf16[6144,128]{1,0:T(8,128)(2,1)} copy(bf16[6144,128]{1,0:T(8,128)(2,1)S(1)} %bitcast.13) | data formatting | bytes 3145728
Async XLA Ops:
  1.4 0.7 copy-start
  2.1 0.7 copy-start.1

commit v4 on v3

--- a/solution.py
+++ b/solution.py
@@ -85,7 +85,7 @@
 
     def local_row(row, carry):
         for k in range(h_ref.shape[1]):
-            at = h_cols[row, k] - me * rows + reach
+            at = h_cols[k, row] - me * rows + reach
             at = jnp.where(at < 0, at + total_rows, at)
             at = jnp.where(at >= total_rows, at - total_rows, at)
             cols[row, k] = jnp.clip(at, 0, rows + 2 * reach - 1)
@@ -205,6 +205,47 @@
     own.wait()
     next_store.wait()
     last_store.wait()
+
+
+def in_hbm(array):
+    return pltpu.with_memory_space_constraint(array, pltpu.HBM)
+
+
+def finish_kernel(steps, next_ref, last_ref, arrived, next_out, last_out, owned, sems):
+    copies = [
+        pltpu.make_async_copy(next_ref, next_out, sems.at[0]),
+        pltpu.make_async_copy(last_ref, last_out, sems.at[1]),
+    ]
+
+    @pl.when(pl.program_id(0) == 0)
+    def _():
+        for c in copies:
+            c.start()
+
+    owned[...] = arrived[...].astype(owned.dtype)
+
+    @pl.when(pl.program_id(0) == steps - 1)
+    def _():
+        for c in copies:
+            c.wait()
+
+
+def finish(made_next, made_last, arrived):
+    devices, span, bs = arrived.shape
+    steps = 4
+    anyspec = pl.BlockSpec(memory_space=pl.ANY)
+    block = pl.BlockSpec((devices // steps, span, bs), lambda i: (i, 0, 0))
+    term = jax.ShapeDtypeStruct(made_next.shape, made_next.dtype)
+    return pl.pallas_call(
+        functools.partial(finish_kernel, steps),
+        out_shape=(term, term, jax.ShapeDtypeStruct(arrived.shape, jnp.float32)),
+        grid=(steps,),
+        in_specs=[anyspec, anyspec, block],
+        out_specs=(anyspec, anyspec, block),
+        scratch_shapes=[pltpu.SemaphoreType.DMA((2,))],
+        compiler_params=pltpu.CompilerParams(vmem_limit_bytes=16 * 1024 * 1024),
+        name="finish",
+    )(made_next, made_last, arrived)
 
 
 def on_device(h_blocks, h_cols, t_prev, t_cur, cheb_coeffs, owner_slot):
@@ -251,14 +292,15 @@
         compiler_params=pltpu.CompilerParams(collective_id=0, has_side_effects=True, vmem_limit_bytes=42 * 1024 * 1024),
         name="whole",
     )(
-        h_cols,
-        cheb_coeffs,
-        owner_slot[None, :],
+        in_hbm(h_cols.T),
+        in_hbm(cheb_coeffs),
+        in_hbm(owner_slot[None, :]),
         h_blocks,
-        pltpu.with_memory_space_constraint(t_prev.reshape(rows, bs, width), pltpu.HBM),
-        pltpu.with_memory_space_constraint(t_cur.reshape(rows, bs, width), pltpu.HBM),
-    )
-    owned = arrived.astype(jnp.float32).reshape(devices * rows, per_dev, bs)
+        in_hbm(t_prev.reshape(rows, bs, width)),
+        in_hbm(t_cur.reshape(rows, bs, width)),
+    )
+    made_next, made_last, owned = finish(made_next, made_last, arrived)
+    owned = owned.reshape(devices * rows, per_dev, bs)
     owned = owned.transpose(1, 0, 2).reshape(per_dev, devices * rows * bs)
     return (made_next.reshape(-1, width), made_last.reshape(-1, width), owned)
 

time: 109 us -> 106 us (0.972)
  local copies, waits for them, and re-layouts: 4.37 us -> 0 us
  Pallas kernels: 102 us -> 105 us
  other arithmetic: 2.03 us -> 0 us
    unnamed x7 -> x0, local copies, waits for them, and re-layouts: 4.37 us -> none
    pallas_call x0 -> x1, Pallas kernels: none -> 3.15 us  [finish(): pl.pallas_call(functools.partial(finish_kernel, steps), out_shape=(term,...]
    unnamed x1 -> x0, other arithmetic: 2.03 us -> none
where the time goes in v4:
time: 106 us
  Pallas kernels  105 us (99%)
    pallas_call x1, Pallas kernels, on_device(): pl.pallas_call(functools.partial(whole_kernel, (reach, pieces, per_dev, g...  102 us
    pallas_call x1, Pallas kernels, finish(): pl.pallas_call(functools.partial(finish_kernel, steps), out_shape=(term,...  3.15 us

profile of v4, /device:TPU:16, one launch (start us, length us, event | category | flops | bytes accessed | tf_op | source)
XLA Modules:
  0.0 105.7 jit_solution(12687414081713192953)
XLA Ops:
  0.6 102.0 %whole.1 = (bf16[48,128,128]{2,1,0:T(8,128)(2,1)S(1)}, bf16[48,128,128]{2,1,0:T(8,128)(2,1)S(1)}, bf16[32,192,128]{2,1,0:T(8,128)(2,1)S(1)}) custom-call(s32[16,48]{1,0:T(8,128)} %bitcast.13, f32[3]{0:T(128)} %coeffs.1, s32[1,128]{1,0:T(1,128)} %bitcast.14, bf16[48,16,128,128]{3,2,1,0:T(8,128)(2,1)} %h_hbm.1, bf16[48,128,128]{2,1,0:T(8,128)(2,1)} %bitcast.11, ...), custom_call_target="tpu_custom_call" | custom-call | tf_op jit(solution)/shard_map/whole/pallas_call | solution.py:268
  102.6 3.2 %finish.1 = (bf16[48,128,128]{2,1,0:T(8,128)(2,1)}, bf16[48,128,128]{2,1,0:T(8,128)(2,1)}, f32[32,192,128]{2,1,0:T(8,128)}) custom-call(bf16[48,128,128]{2,1,0:T(8,128)(2,1)S(1)} %get-tuple-element.9.next_ref, bf16[48,128,128]{2,1,0:T(8,128)(2,1)S(1)} %get-tuple-element.10.last_ref, bf16[32,192,128]{2,1,0:T(8,128)(2,1)S(1)} %get-tuple-element.11.arrived), custom_call_target="tpu_custom_call" | custom-call | tf_op jit(solution)/shard_map/finish/pallas_call | solution.py:239
